TPU v7x, 256 devices: a whole 4x4x8 slice. The times are simulated.
256 devices in a mesh: frow: 8 (over z_lo, core), fcol: 32 (over x, z_hi, y).
Axes of the slice: x: 4, y: 4, z: 8 (z_hi: 2, z_lo: 4; z = z_hi * 4 + z_lo), core: 2. Of those that a mesh axis runs over, the one named last changes fastest.
Arguments:
- right_side: float32 [64, 1024, 256], P('frow', 'fcol'), may hold values from -6 to 6
- noise_weight: float32 [64, 1024, 256], P('frow', 'fcol'), may hold values from 3 to 4.5
- stencils: bfloat16 [9, 256, 256], replicated, may hold values from -1 to 1, as said below
- neighbours: int32 [64, 1024, 9], P('frow', 'fcol'), may hold values from -1 to 65535, as said below
Outputs:
- solution: float32 [64, 1024, 256], P('frow', 'fcol')
- coarse_residual: float32 [32, 512, 256], P('frow')
Inputs may be any that keep to these rules, and one draw needn't show every extreme that they name: `neighbours`: each entry is -1 (an empty slot) or the index r * 1024 + c of the tile at row r = own row + k // 3 - 1 and column c = own column + k % 3 - 1 for slot k; slot 4 always holds the tile itself; if tile t holds tile s in slot k, then s holds t in slot 8 - k. stencils[8 - k] is the transpose of stencils[k], and stencils[4] is symmetric.
All inputs are finite; a program needn't handle non-finite values.
Results may differ from a plain program's by a relative error of at most 0.0031.
Values may be sent and summed in bfloat16 or wider, within the bound.
A program may use at most 64 MiB of HBM per device.

v0:
```python
import jax
import jax.numpy as jnp
from jax import lax
from jax.sharding import PartitionSpec as P

DEG = 3
lower_edge = 1.5
upper_edge = 6.0


def with_halo(cells, sides, width):
    for axis, dim in sides:
        count = lax.axis_size(axis)
        ends = count - 1
        head = lax.slice_in_dim(cells, 0, width, axis=dim)
        tail = lax.slice_in_dim(cells, cells.shape[dim] - width, cells.shape[dim], axis=dim)
        cells = jnp.concatenate(
            [
                lax.ppermute(tail, axis, [(i, (i + 1) % count) for i in range(ends)]),
                cells,
                lax.ppermute(head, axis, [((i + 1) % count, i) for i in range(ends)]),
            ],
            axis=dim,
        )
    return cells


def restrict(paired_block):
    height, width, doubled = paired_block.shape
    pixels = doubled // 2
    summed = jnp.sum(paired_block.reshape(height // 2, 2, width, 2, pixels // 4, 4), axis=5)
    return jnp.transpose(summed, (0, 2, 1, 3, 4)).reshape(height // 2, width, pixels)


def smooth(right_side, operate):
    center = 0.5 * (upper_edge + lower_edge)
    half_width = 0.5 * (upper_edge - lower_edge)
    spread_ratio = center / half_width
    solution = jnp.zeros_like(right_side)
    residual = right_side
    for sweep_index in range(2):
        ratio_now = 1.0 / spread_ratio
        direction = residual / center
        for step_index in range(DEG):
            solution = solution + direction
            residual = residual - operate(direction)
            if step_index < DEG - 1:
                ratio_next = 1.0 / (2.0 * spread_ratio - ratio_now)
                direction = (
                    ratio_next * ratio_now * direction + 2.0 * ratio_next / half_width * residual
                )
                ratio_now = ratio_next
    return (solution, residual)


def body(right_side, noise_weight, stencils, neighbours):
    tile_rows, tile_cols, pixels = right_side.shape
    slots = stencils.shape[0]
    grid_cols = tile_cols * lax.axis_size("fcol")
    row_anchor = lax.axis_index("frow") * tile_rows
    col_anchor = lax.axis_index("fcol") * tile_cols
    padded_count = (tile_rows + 2) * (tile_cols + 2)
    local_row = neighbours // grid_cols - row_anchor + 1
    local_col = neighbours % grid_cols - col_anchor + 1
    targets = jnp.where(
        neighbours < 0, padded_count, local_row * (tile_cols + 2) + local_col
    ).reshape(-1)
    stencil_matrix = stencils.reshape(slots * pixels, pixels)

    def operate(direction):
        rounded = direction.astype(jnp.bfloat16)
        padded = with_halo(rounded, (("frow", 0), ("fcol", 1)), 1)
        flattened = jnp.concatenate(
            [padded.reshape(padded_count, pixels), jnp.zeros((1, pixels), jnp.bfloat16)], 0
        )
        picked = jnp.take(flattened, targets, axis=0).reshape(tile_rows * tile_cols, slots * pixels)
        coupled = jnp.dot(picked, stencil_matrix, preferred_element_type=jnp.float32)
        return noise_weight * direction + coupled.reshape(tile_rows, tile_cols, pixels)

    solution, residual = smooth(right_side, operate)
    paired = residual.reshape(tile_rows, tile_cols // 2, 2 * pixels)
    coarse_residual = lax.all_gather(restrict(paired), "fcol", axis=1, tiled=True)
    return (solution, coarse_residual)


def solution(mesh):
    placed = (P("frow", "fcol", None), P("frow", "fcol", None), P(), P("frow", "fcol", None))
    return jax.shard_map(
        body,
        mesh=mesh,
        in_specs=placed,
        out_specs=(P("frow", "fcol", None), P("frow", None, None)),
        check_vma=False,
    )
```

profile of v0, /device:TPU:2, one launch (start us, length us, event | category | flops | bytes accessed | tf_op | source)
XLA Modules:
  0.0 339.4 jit_solution(16433742648850729699)
XLA Ops:
  12.5 2.3 collective-permute-done.1
  14.9 3.5 %collective-permute-start.2 = (bf16[10,1,256]{2,1,0:T(2,128)(2,1)S(1)}, bf16[10,1,256]{2,1,0:T(2,128)(2,1)S(1)}, u32[]{:S(2)}, u32[]{:S(2)}) collective-permute-start(bf16[10,1,256]{2,1,0:T(2,128)(2,1)S(1)} %get-tuple-element.15), channel_id=1, source_target_pairs={{0,1},{1,2},{2,3},{3,4},{4,5},{5,6},{6,7},{7,8},{8,9},{9,10},{10,1... | collective-permute-start | bytes 15368 | tf_op jit(solution)/shard_map/ppermute | solution.py:19
  18.3 9.3 %collective-permute-start.3 = (bf16[10,1,256]{2,1,0:T(2,128)(2,1)S(1)}, bf16[10,1,256]{2,1,0:T(2,128)(2,1)S(1)}, u32[]{:S(2)}, u32[]{:S(2)}) collective-permute-start(bf16[10,1,256]{2,1,0:T(2,128)(2,1)S(1)} %get-tuple-element.16), channel_id=1, source_target_pairs={{1,0},{2,1},{3,2},{4,3},{5,4},{6,5},{7,6},{8,7},{9,8},{10,9},{11,1... | collective-permute-start | bytes 15368 | tf_op jit(solution)/shard_map/ppermute | solution.py:21
  29.2 6.9 %gather_fusion = bf16[2304,256]{1,0:T(8,128)(2,1)S(1)} fusion(bf16[341,256]{1,0:T(8,128)(2,1)S(1)} %concatenate.56, s32[3072]{0:T(1024)S(1)} %pad_clamp_fusion), kind=kCustom, calls=%fused_computation.clone | custom fusion | bytes 2368512 | tf_op jit(solution)/shard_map/jit(_take)/gather | solution.py:76
  36.0 2.1 broadcast_select_fusion.5
  38.1 2.7 dot_general.30
  41.3 3.3 collective-permute-start.4
  46.0 2.4 collective-permute-done.5
  48.4 1.9 collective-permute-start.6
  50.3 11.1 %collective-permute-start.7 = (bf16[10,1,256]{2,1,0:T(2,128)(2,1)S(1)}, bf16[10,1,256]{2,1,0:T(2,128)(2,1)S(1)}, u32[]{:S(2)}, u32[]{:S(2)}) collective-permute-start(bf16[10,1,256]{2,1,0:T(2,128)(2,1)S(1)} %get-tuple-element.14), channel_id=1, source_target_pairs={{1,0},{2,1},{3,2},{4,3},{5,4},{6,5},{7,6},{8,7},{9,8},{10,9},{11,1... | collective-permute-start | bytes 15368 | tf_op jit(solution)/shard_map/ppermute | solution.py:21
  63.0 6.9 %gather_fusion.1 = bf16[2304,256]{1,0:T(8,128)(2,1)S(1)} fusion(bf16[341,256]{1,0:T(8,128)(2,1)S(1)} %concatenate.59, s32[3072]{0:T(1024)S(1)} %pad_clamp_fusion), kind=kCustom, calls=%fused_computation.1.clone | custom fusion | bytes 2368512 | tf_op jit(solution)/shard_map/jit(_take)/gather | solution.py:76
  69.8 2.1 broadcast_select_fusion.4
  71.9 2.7 dot_general.32
  75.8 3.5 %collective-permute-start.8 = (bf16[1,32,256]{2,1,0:T(8,128)(2,1)S(1)}, bf16[1,32,256]{2,1,0:T(8,128)(2,1)S(1)}, u32[]{:S(2)}, u32[]{:S(2)}) collective-permute-start(bf16[1,32,256]{2,1,0:T(8,128)(2,1)S(1)} %get-tuple-element.23), channel_id=1, source_target_pairs={{0,32},{32,64},{64,96},{96,128},{128,160},{160,192},{192,224},{1,3... | collective-permute-start | bytes 49160 | tf_op jit(solution)/shard_map/ppermute | solution.py:19
  80.6 2.2 collective-permute-done.9
  82.8 2.7 collective-permute-start.10
  85.5 10.3 %collective-permute-start.11 = (bf16[10,1,256]{2,1,0:T(2,128)(2,1)S(1)}, bf16[10,1,256]{2,1,0:T(2,128)(2,1)S(1)}, u32[]{:S(2)}, u32[]{:S(2)}) collective-permute-start(bf16[10,1,256]{2,1,0:T(2,128)(2,1)S(1)} %get-tuple-element.12), channel_id=1, source_target_pairs={{1,0},{2,1},{3,2},{4,3},{5,4},{6,5},{7,6},{8,7},{9,8},{10,9},{11,1... | collective-permute-start | bytes 15368 | tf_op jit(solution)/shard_map/ppermute | solution.py:21
  97.4 7.5 %gather_fusion.2 = bf16[2304,256]{1,0:T(8,128)(2,1)} fusion(bf16[341,256]{1,0:T(8,128)(2,1)S(1)} %concatenate.62, s32[3072]{0:T(1024)S(1)} %pad_clamp_fusion), kind=kCustom, calls=%fused_computation.2.clone | custom fusion | bytes 2368512 | tf_op jit(solution)/shard_map/jit(_take)/gather | solution.py:76
  104.8 2.3 broadcast_select_fusion.3
  107.1 2.1 dot_general.34
  109.2 1.9 multiply_convert_fusion
  111.1 3.5 %collective-permute-start.12 = (bf16[1,32,256]{2,1,0:T(8,128)(2,1)S(1)}, bf16[1,32,256]{2,1,0:T(8,128)(2,1)S(1)}, u32[]{:S(2)}, u32[]{:S(2)}) collective-permute-start(bf16[1,32,256]{2,1,0:T(8,128)(2,1)S(1)} %get-tuple-element.21), channel_id=1, source_target_pairs={{0,32},{32,64},{64,96},{96,128},{128,160},{160,192},{192,224},{1,3... | collective-permute-start | bytes 49160 | tf_op jit(solution)/shard_map/ppermute | solution.py:19
  115.9 2.2 collective-permute-done.13
  118.1 1.9 collective-permute-start.14
  120.0 11.3 %collective-permute-start.15 = (bf16[10,1,256]{2,1,0:T(2,128)(2,1)S(1)}, bf16[10,1,256]{2,1,0:T(2,128)(2,1)S(1)}, u32[]{:S(2)}, u32[]{:S(2)}) collective-permute-start(bf16[10,1,256]{2,1,0:T(2,128)(2,1)S(1)} %get-tuple-element.10), channel_id=1, source_target_pairs={{1,0},{2,1},{3,2},{4,3},{5,4},{6,5},{7,6},{8,7},{9,8},{10,9},{11,1... | collective-permute-start | bytes 15368 | tf_op jit(solution)/shard_map/ppermute | solution.py:21
  132.7 6.9 %gather_fusion.3 = bf16[2304,256]{1,0:T(8,128)(2,1)S(1)} fusion(bf16[341,256]{1,0:T(8,128)(2,1)S(1)} %concatenate.65, s32[3072]{0:T(1024)S(1)} %pad_clamp_fusion), kind=kCustom, calls=%fused_computation.3.clone | custom fusion | bytes 2368512 | tf_op jit(solution)/shard_map/jit(_take)/gather | solution.py:76
  139.5 2.1 broadcast_select_fusion.2
  141.6 2.7 dot_general.36
  145.5 3.5 %collective-permute-start.16 = (bf16[1,32,256]{2,1,0:T(8,128)(2,1)S(1)}, bf16[1,32,256]{2,1,0:T(8,128)(2,1)S(1)}, u32[]{:S(2)}, u32[]{:S(2)}) collective-permute-start(bf16[1,32,256]{2,1,0:T(8,128)(2,1)S(1)} %get-tuple-element.19), channel_id=1, source_target_pairs={{0,32},{32,64},{64,96},{96,128},{128,160},{160,192},{192,224},{1,3... | collective-permute-start | bytes 49160 | tf_op jit(solution)/shard_map/ppermute | solution.py:19
  150.3 2.2 collective-permute-done.17
  152.5 1.9 collective-permute-start.18
  154.4 11.1 %collective-permute-start.19 = (bf16[10,1,256]{2,1,0:T(2,128)(2,1)S(1)}, bf16[10,1,256]{2,1,0:T(2,128)(2,1)S(1)}, u32[]{:S(2)}, u32[]{:S(2)}) collective-permute-start(bf16[10,1,256]{2,1,0:T(2,128)(2,1)S(1)} %get-tuple-element.8), channel_id=1, source_target_pairs={{1,0},{2,1},{3,2},{4,3},{5,4},{6,5},{7,6},{8,7},{9,8},{10,9},{11,1... | collective-permute-start | bytes 15368 | tf_op jit(solution)/shard_map/ppermute | solution.py:21
  167.0 6.9 %gather_fusion.4 = bf16[2304,256]{1,0:T(8,128)(2,1)S(1)} fusion(bf16[341,256]{1,0:T(8,128)(2,1)S(1)} %concatenate.68, s32[3072]{0:T(1024)S(1)} %pad_clamp_fusion), kind=kCustom, calls=%fused_computation.4.clone | custom fusion | bytes 2368512 | tf_op jit(solution)/shard_map/jit(_take)/gather | solution.py:76
  173.9 2.1 broadcast_select_fusion.1
  176.0 2.7 dot_general.38
  178.6 2.5 fusion.7
  181.1 3.5 %collective-permute-start.20 = (bf16[1,32,256]{2,1,0:T(8,128)(2,1)S(1)}, bf16[1,32,256]{2,1,0:T(8,128)(2,1)S(1)}, u32[]{:S(2)}, u32[]{:S(2)}) collective-permute-start(bf16[1,32,256]{2,1,0:T(8,128)(2,1)S(1)} %get-tuple-element.17), channel_id=1, source_target_pairs={{0,32},{32,64},{64,96},{96,128},{128,160},{160,192},{192,224},{1,3... | collective-permute-start | bytes 49160 | tf_op jit(solution)/shard_map/ppermute | solution.py:19
  185.9 2.2 collective-permute-done.21
  188.1 1.9 collective-permute-start.22
  190.0 11.3 %collective-permute-start.23 = (bf16[10,1,256]{2,1,0:T(2,128)(2,1)S(1)}, bf16[10,1,256]{2,1,0:T(2,128)(2,1)S(1)}, u32[]{:S(2)}, u32[]{:S(2)}) collective-permute-start(bf16[10,1,256]{2,1,0:T(2,128)(2,1)S(1)} %get-tuple-element.6), channel_id=1, source_target_pairs={{1,0},{2,1},{3,2},{4,3},{5,4},{6,5},{7,6},{8,7},{9,8},{10,9},{11,1... | collective-permute-start | bytes 15368 | tf_op jit(solution)/shard_map/ppermute | solution.py:21
  202.7 6.9 %gather_fusion.5 = bf16[2304,256]{1,0:T(8,128)(2,1)S(1)} fusion(bf16[341,256]{1,0:T(8,128)(2,1)S(1)} %concatenate.71, s32[3072]{0:T(1024)S(1)} %pad_clamp_fusion), kind=kCustom, calls=%fused_computation.5.clone | custom fusion | bytes 2368512 | tf_op jit(solution)/shard_map/jit(_take)/gather | solution.py:76
  209.6 2.1 broadcast_select_fusion
  211.6 2.7 dot_general.40
  214.3 2.1 fusion
  216.5 10.9 %reshape_reshape.3 = f32[4,2,16,2,64,4]{5,4,3,2,1,0:T(8,128)} reshape(f32[8,32,256]{2,1,0:T(8,128)} %fusion) | data formatting | bytes 524288 | tf_op jit(solution)/shard_map/reshape;reshape | solution.py:31
  227.4 5.7 %reduce_sum.9 = f32[4,2,16,2,64]{4,3,2,1,0:T(2,128)S(1)} reduce(f32[4,2,16,2,64,4]{5,4,3,2,1,0:T(8,128)} %reshape_reshape.3, f32[]{:T(128)} %constant.74.clone.1), dimensions={5}, to_apply=%region_0.2 | reduce | flops 49152 | bytes 327684 | tf_op jit(solution)/shard_map/reduce_sum | solution.py:31
  233.9 95.6 %all-gather.2.cloned.1.call-done = f32[4,512,256]{2,1,0:T(8,128)} async-done(((f32[4,16,256]{2,1,0:T(8,128)}), f32[4,512,256]{2,1,0:T(8,128)}) %all-gather.2.cloned.1.call-update) | async-done | bytes 2097168 | tf_op jit(solution)/shard_map/all_gather | solution.py:82
  329.5 3.0 copy.11
  (79 shorter events, 24.3 us)
Async XLA Ops:
  7.2 33.6 %copy-start = (bf16[9,256,256]{2,1,0:T(8,128)(2,1)S(1)}, bf16[9,256,256]{2,1,0:T(8,128)(2,1)}, u32[]{:S(2)}) copy-start(bf16[9,256,256]{2,1,0:T(8,128)(2,1)} %param.8) | copy-start | bytes 3538948
  7.2 322.3 %all-gather.2.cloned.1.call-start = ((), (), s32[]{:S(2)}) async-start(), calls=%async_computation | async-start | bytes 2162688 | tf_op jit(solution)/shard_map/all_gather | solution.py:82
  8.3 4.2 %collective-permute-start = (bf16[1,32,256]{2,1,0:T(8,128)(2,1)S(1)}, bf16[1,32,256]{2,1,0:T(8,128)(2,1)S(1)}, u32[]{:S(2)}, u32[]{:S(2)}) collective-permute-start(bf16[1,32,256]{2,1,0:T(8,128)(2,1)S(1)} %get-tuple-element.27), channel_id=1, source_target_pairs={{0,32},{32,64},{64,96},{96,128},{128,160},{160,192},{192,224},{1,3... | collective-permute-start | bytes 49160 | tf_op jit(solution)/shard_map/ppermute | solution.py:19
  10.0 4.8 %collective-permute-start.1 = (bf16[1,32,256]{2,1,0:T(8,128)(2,1)S(1)}, bf16[1,32,256]{2,1,0:T(8,128)(2,1)S(1)}, u32[]{:S(2)}, u32[]{:S(2)}) collective-permute-start(bf16[1,32,256]{2,1,0:T(8,128)(2,1)S(1)} %get-tuple-element.28), channel_id=1, source_target_pairs={{32,0},{64,32},{96,64},{128,96},{160,128},{192,160},{224,192},{33,... | collective-permute-start | bytes 49160 | tf_op jit(solution)/shard_map/ppermute | solution.py:21
  14.9 12.8 %collective-permute-start.2 = (bf16[10,1,256]{2,1,0:T(2,128)(2,1)S(1)}, bf16[10,1,256]{2,1,0:T(2,128)(2,1)S(1)}, u32[]{:S(2)}, u32[]{:S(2)}) collective-permute-start(bf16[10,1,256]{2,1,0:T(2,128)(2,1)S(1)} %get-tuple-element.15), channel_id=1, source_target_pairs={{0,1},{1,2},{2,3},{3,4},{4,5},{5,6},{6,7},{7,8},{8,9},{9,10},{10,1... | collective-permute-start | bytes 15368 | tf_op jit(solution)/shard_map/ppermute | solution.py:19
  18.3 10.6 %collective-permute-start.3 = (bf16[10,1,256]{2,1,0:T(2,128)(2,1)S(1)}, bf16[10,1,256]{2,1,0:T(2,128)(2,1)S(1)}, u32[]{:S(2)}, u32[]{:S(2)}) collective-permute-start(bf16[10,1,256]{2,1,0:T(2,128)(2,1)S(1)} %get-tuple-element.16), channel_id=1, source_target_pairs={{1,0},{2,1},{3,2},{4,3},{5,4},{6,5},{7,6},{8,7},{9,8},{10,9},{11,1... | collective-permute-start | bytes 15368 | tf_op jit(solution)/shard_map/ppermute | solution.py:21
  38.1 2.7 copy-start.1
  38.1 2.7 copy-start.2
  41.3 33.2 %copy-start.3 = (f32[8,32,256]{2,1,0:T(8,128)}, f32[8,32,256]{2,1,0:T(8,128)S(1)}, u32[]{:S(2)}) copy-start(f32[8,32,256]{2,1,0:T(8,128)S(1)} %get-tuple-element.30) | copy-start | bytes 786436
  41.3 4.6 %collective-permute-start.4 = (bf16[1,32,256]{2,1,0:T(8,128)(2,1)S(1)}, bf16[1,32,256]{2,1,0:T(8,128)(2,1)S(1)}, u32[]{:S(2)}, u32[]{:S(2)}) collective-permute-start(bf16[1,32,256]{2,1,0:T(8,128)(2,1)S(1)} %get-tuple-element.25), channel_id=1, source_target_pairs={{0,32},{32,64},{64,96},{96,128},{128,160},{160,192},{192,224},{1,3... | collective-permute-start | bytes 49160 | tf_op jit(solution)/shard_map/ppermute | solution.py:19
  44.7 3.7 %collective-permute-start.5 = (bf16[1,32,256]{2,1,0:T(8,128)(2,1)S(1)}, bf16[1,32,256]{2,1,0:T(8,128)(2,1)S(1)}, u32[]{:S(2)}, u32[]{:S(2)}) collective-permute-start(bf16[1,32,256]{2,1,0:T(8,128)(2,1)S(1)} %get-tuple-element.26), channel_id=1, source_target_pairs={{32,0},{64,32},{96,64},{128,96},{160,128},{192,160},{224,192},{33,... | collective-permute-start | bytes 49160 | tf_op jit(solution)/shard_map/ppermute | solution.py:21
  48.4 13.1 %collective-permute-start.6 = (bf16[10,1,256]{2,1,0:T(2,128)(2,1)S(1)}, bf16[10,1,256]{2,1,0:T(2,128)(2,1)S(1)}, u32[]{:S(2)}, u32[]{:S(2)}) collective-permute-start(bf16[10,1,256]{2,1,0:T(2,128)(2,1)S(1)} %get-tuple-element.13), channel_id=1, source_target_pairs={{0,1},{1,2},{2,3},{3,4},{4,5},{5,6},{6,7},{7,8},{8,9},{9,10},{10,1... | collective-permute-start | bytes 15368 | tf_op jit(solution)/shard_map/ppermute | solution.py:19
  50.3 12.5 %collective-permute-start.7 = (bf16[10,1,256]{2,1,0:T(2,128)(2,1)S(1)}, bf16[10,1,256]{2,1,0:T(2,128)(2,1)S(1)}, u32[]{:S(2)}, u32[]{:S(2)}) collective-permute-start(bf16[10,1,256]{2,1,0:T(2,128)(2,1)S(1)} %get-tuple-element.14), channel_id=1, source_target_pairs={{1,0},{2,1},{3,2},{4,3},{5,4},{6,5},{7,6},{8,7},{9,8},{10,9},{11,1... | collective-permute-start | bytes 15368 | tf_op jit(solution)/shard_map/ppermute | solution.py:21
  75.8 4.8 %collective-permute-start.8 = (bf16[1,32,256]{2,1,0:T(8,128)(2,1)S(1)}, bf16[1,32,256]{2,1,0:T(8,128)(2,1)S(1)}, u32[]{:S(2)}, u32[]{:S(2)}) collective-permute-start(bf16[1,32,256]{2,1,0:T(8,128)(2,1)S(1)} %get-tuple-element.23), channel_id=1, source_target_pairs={{0,32},{32,64},{64,96},{96,128},{128,160},{160,192},{192,224},{1,3... | collective-permute-start | bytes 49160 | tf_op jit(solution)/shard_map/ppermute | solution.py:19
  79.3 3.5 %collective-permute-start.9 = (bf16[1,32,256]{2,1,0:T(8,128)(2,1)S(1)}, bf16[1,32,256]{2,1,0:T(8,128)(2,1)S(1)}, u32[]{:S(2)}, u32[]{:S(2)}) collective-permute-start(bf16[1,32,256]{2,1,0:T(8,128)(2,1)S(1)} %get-tuple-element.24), channel_id=1, source_target_pairs={{32,0},{64,32},{96,64},{128,96},{160,128},{192,160},{224,192},{33,... | collective-permute-start | bytes 49160 | tf_op jit(solution)/shard_map/ppermute | solution.py:21
  82.8 13.1 %collective-permute-start.10 = (bf16[10,1,256]{2,1,0:T(2,128)(2,1)S(1)}, bf16[10,1,256]{2,1,0:T(2,128)(2,1)S(1)}, u32[]{:S(2)}, u32[]{:S(2)}) collective-permute-start(bf16[10,1,256]{2,1,0:T(2,128)(2,1)S(1)} %get-tuple-element.11), channel_id=1, source_target_pairs={{0,1},{1,2},{2,3},{3,4},{4,5},{5,6},{6,7},{7,8},{8,9},{9,10},{10,1... | collective-permute-start | bytes 15368 | tf_op jit(solution)/shard_map/ppermute | solution.py:19
  85.5 11.7 %collective-permute-start.11 = (bf16[10,1,256]{2,1,0:T(2,128)(2,1)S(1)}, bf16[10,1,256]{2,1,0:T(2,128)(2,1)S(1)}, u32[]{:S(2)}, u32[]{:S(2)}) collective-permute-start(bf16[10,1,256]{2,1,0:T(2,128)(2,1)S(1)} %get-tuple-element.12), channel_id=1, source_target_pairs={{1,0},{2,1},{3,2},{4,3},{5,4},{6,5},{7,6},{8,7},{9,8},{10,9},{11,1... | collective-permute-start | bytes 15368 | tf_op jit(solution)/shard_map/ppermute | solution.py:21
  111.1 4.8 %collective-permute-start.12 = (bf16[1,32,256]{2,1,0:T(8,128)(2,1)S(1)}, bf16[1,32,256]{2,1,0:T(8,128)(2,1)S(1)}, u32[]{:S(2)}, u32[]{:S(2)}) collective-permute-start(bf16[1,32,256]{2,1,0:T(8,128)(2,1)S(1)} %get-tuple-element.21), channel_id=1, source_target_pairs={{0,32},{32,64},{64,96},{96,128},{128,160},{160,192},{192,224},{1,3... | collective-permute-start | bytes 49160 | tf_op jit(solution)/shard_map/ppermute | solution.py:19
  114.6 3.5 %collective-permute-start.13 = (bf16[1,32,256]{2,1,0:T(8,128)(2,1)S(1)}, bf16[1,32,256]{2,1,0:T(8,128)(2,1)S(1)}, u32[]{:S(2)}, u32[]{:S(2)}) collective-permute-start(bf16[1,32,256]{2,1,0:T(8,128)(2,1)S(1)} %get-tuple-element.22), channel_id=1, source_target_pairs={{32,0},{64,32},{96,64},{128,96},{160,128},{192,160},{224,192},{33,... | collective-permute-start | bytes 49160 | tf_op jit(solution)/shard_map/ppermute | solution.py:21
  118.1 13.2 %collective-permute-start.14 = (bf16[10,1,256]{2,1,0:T(2,128)(2,1)S(1)}, bf16[10,1,256]{2,1,0:T(2,128)(2,1)S(1)}, u32[]{:S(2)}, u32[]{:S(2)}) collective-permute-start(bf16[10,1,256]{2,1,0:T(2,128)(2,1)S(1)} %get-tuple-element.9), channel_id=1, source_target_pairs={{0,1},{1,2},{2,3},{3,4},{4,5},{5,6},{6,7},{7,8},{8,9},{9,10},{10,1... | collective-permute-start | bytes 15368 | tf_op jit(solution)/shard_map/ppermute | solution.py:19
  120.0 12.5 %collective-permute-start.15 = (bf16[10,1,256]{2,1,0:T(2,128)(2,1)S(1)}, bf16[10,1,256]{2,1,0:T(2,128)(2,1)S(1)}, u32[]{:S(2)}, u32[]{:S(2)}) collective-permute-start(bf16[10,1,256]{2,1,0:T(2,128)(2,1)S(1)} %get-tuple-element.10), channel_id=1, source_target_pairs={{1,0},{2,1},{3,2},{4,3},{5,4},{6,5},{7,6},{8,7},{9,8},{10,9},{11,1... | collective-permute-start | bytes 15368 | tf_op jit(solution)/shard_map/ppermute | solution.py:21
  145.5 4.8 %collective-permute-start.16 = (bf16[1,32,256]{2,1,0:T(8,128)(2,1)S(1)}, bf16[1,32,256]{2,1,0:T(8,128)(2,1)S(1)}, u32[]{:S(2)}, u32[]{:S(2)}) collective-permute-start(bf16[1,32,256]{2,1,0:T(8,128)(2,1)S(1)} %get-tuple-element.19), channel_id=1, source_target_pairs={{0,32},{32,64},{64,96},{96,128},{128,160},{160,192},{192,224},{1,3... | collective-permute-start | bytes 49160 | tf_op jit(solution)/shard_map/ppermute | solution.py:19
  149.0 3.5 %collective-permute-start.17 = (bf16[1,32,256]{2,1,0:T(8,128)(2,1)S(1)}, bf16[1,32,256]{2,1,0:T(8,128)(2,1)S(1)}, u32[]{:S(2)}, u32[]{:S(2)}) collective-permute-start(bf16[1,32,256]{2,1,0:T(8,128)(2,1)S(1)} %get-tuple-element.20), channel_id=1, source_target_pairs={{32,0},{64,32},{96,64},{128,96},{160,128},{192,160},{224,192},{33,... | collective-permute-start | bytes 49160 | tf_op jit(solution)/shard_map/ppermute | solution.py:21
  152.5 13.0 %collective-permute-start.18 = (bf16[10,1,256]{2,1,0:T(2,128)(2,1)S(1)}, bf16[10,1,256]{2,1,0:T(2,128)(2,1)S(1)}, u32[]{:S(2)}, u32[]{:S(2)}) collective-permute-start(bf16[10,1,256]{2,1,0:T(2,128)(2,1)S(1)} %get-tuple-element.7), channel_id=1, source_target_pairs={{0,1},{1,2},{2,3},{3,4},{4,5},{5,6},{6,7},{7,8},{8,9},{9,10},{10,1... | collective-permute-start | bytes 15368 | tf_op jit(solution)/shard_map/ppermute | solution.py:19
  154.4 12.5 %collective-permute-start.19 = (bf16[10,1,256]{2,1,0:T(2,128)(2,1)S(1)}, bf16[10,1,256]{2,1,0:T(2,128)(2,1)S(1)}, u32[]{:S(2)}, u32[]{:S(2)}) collective-permute-start(bf16[10,1,256]{2,1,0:T(2,128)(2,1)S(1)} %get-tuple-element.8), channel_id=1, source_target_pairs={{1,0},{2,1},{3,2},{4,3},{5,4},{6,5},{7,6},{8,7},{9,8},{10,9},{11,1... | collective-permute-start | bytes 15368 | tf_op jit(solution)/shard_map/ppermute | solution.py:21
  181.1 4.8 %collective-permute-start.20 = (bf16[1,32,256]{2,1,0:T(8,128)(2,1)S(1)}, bf16[1,32,256]{2,1,0:T(8,128)(2,1)S(1)}, u32[]{:S(2)}, u32[]{:S(2)}) collective-permute-start(bf16[1,32,256]{2,1,0:T(8,128)(2,1)S(1)} %get-tuple-element.17), channel_id=1, source_target_pairs={{0,32},{32,64},{64,96},{96,128},{128,160},{160,192},{192,224},{1,3... | collective-permute-start | bytes 49160 | tf_op jit(solution)/shard_map/ppermute | solution.py:19
  184.6 3.5 %collective-permute-start.21 = (bf16[1,32,256]{2,1,0:T(8,128)(2,1)S(1)}, bf16[1,32,256]{2,1,0:T(8,128)(2,1)S(1)}, u32[]{:S(2)}, u32[]{:S(2)}) collective-permute-start(bf16[1,32,256]{2,1,0:T(8,128)(2,1)S(1)} %get-tuple-element.18), channel_id=1, source_target_pairs={{32,0},{64,32},{96,64},{128,96},{160,128},{192,160},{224,192},{33,... | collective-permute-start | bytes 49160 | tf_op jit(solution)/shard_map/ppermute | solution.py:21
  188.1 13.3 %collective-permute-start.22 = (bf16[10,1,256]{2,1,0:T(2,128)(2,1)S(1)}, bf16[10,1,256]{2,1,0:T(2,128)(2,1)S(1)}, u32[]{:S(2)}, u32[]{:S(2)}) collective-permute-start(bf16[10,1,256]{2,1,0:T(2,128)(2,1)S(1)} %get-tuple-element.5), channel_id=1, source_target_pairs={{0,1},{1,2},{2,3},{3,4},{4,5},{5,6},{6,7},{7,8},{8,9},{9,10},{10,1... | collective-permute-start | bytes 15368 | tf_op jit(solution)/shard_map/ppermute | solution.py:19
  190.0 12.5 %collective-permute-start.23 = (bf16[10,1,256]{2,1,0:T(2,128)(2,1)S(1)}, bf16[10,1,256]{2,1,0:T(2,128)(2,1)S(1)}, u32[]{:S(2)}, u32[]{:S(2)}) collective-permute-start(bf16[10,1,256]{2,1,0:T(2,128)(2,1)S(1)} %get-tuple-element.6), channel_id=1, source_target_pairs={{1,0},{2,1},{3,2},{4,3},{5,4},{6,5},{7,6},{8,7},{9,8},{10,9},{11,1... | collective-permute-start | bytes 15368 | tf_op jit(solution)/shard_map/ppermute | solution.py:21
  211.6 2.7 copy-start.4
Sparse Core Ops, SparseCore 0:
  234.1 95.3 all-gather.1
where the time goes:
time: 341 us; the launch traced here: 339 us
  waiting for transfers between devices  117 us (34%)
  starting transfers between devices  105 us (31%)
  local copies, waits for them, and re-layouts  72.8 us (21%)
  other arithmetic  20.7 us (6%)
  between operations  14.7 us (4%)
  matrix products  9.38 us (3%)
    all_gather x1, waiting for transfers between devices, body(): lax.all_gather(restrict(paired), 'fcol', axis=1, tiled=True)  95.6 us
    ppermute x12, starting transfers between devices, with_halo(): lax.ppermute(head, axis, [((i + 1) % count, i) for i in range(ends)])  72.2 us
    gather x6, local copies, waits for them, and re-layouts, operate(): jnp.take(flattened, targets, axis=0)  41.8 us
    ppermute x12, starting transfers between devices, with_halo(): lax.ppermute(tail, axis, [(i, (i + 1) % count) for i in range(ends)])  33 us
    ppermute x12, waiting for transfers between devices, with_halo(): lax.ppermute(head, axis, [((i + 1) % count, i) for i in range(ends)])  21 us
    dot_general x6, local copies, waits for them, and re-layouts, operate(): jnp.dot(picked, stencil_matrix, preferred_element_type=jnp.float32)  15.5 us
    select_n x7, other arithmetic, operate(): jnp.take(flattened, targets, axis=0)  12.6 us
    another operation x1, local copies, waits for them, and re-layouts, restrict(): paired_block.reshape(height // 2, 2, width, 2, pixels // 4, 4)  10.9 us
  transfers between devices with their start and end apart: 25, of which 13 were waited for; matrix products, arithmetic and copies ran while one was open for 0% of the time, Pallas kernels for 0%

commit v1 on v0

--- a/solution.py
+++ b/solution.py
@@ -79,7 +79,9 @@
 
     solution, residual = smooth(right_side, operate)
     paired = residual.reshape(tile_rows, tile_cols // 2, 2 * pixels)
-    coarse_residual = lax.all_gather(restrict(paired), "fcol", axis=1, tiled=True)
+    x = restrict(paired)
+    stack = jnp.stack([x] * lax.axis_size("fcol"))
+    coarse_residual = jnp.concatenate(lax.all_to_all(stack, "fcol", 0, 0), axis=1)
     return (solution, coarse_residual)
 
 

time: 341 us -> 298 us (0.87)
  the two profiles are of different devices: /device:TPU:2 before, /device:TPU:65 now
where the time goes in v1:
time: 298 us; the launch traced here: 296 us
  starting transfers between devices  77.8 us (26%)
  blocking collectives  76.7 us (26%)
  local copies, waits for them, and re-layouts  70.9 us (24%)
  waiting for transfers between devices  39.4 us (13%)
  other arithmetic  20.7 us (7%)
  matrix products  9.37 us (3%)
    all_to_all x1, blocking collectives, body(): lax.all_to_all(stack, 'fcol', 0, 0)  76.7 us
    ppermute x12, starting transfers between devices, with_halo(): lax.ppermute(tail, axis, [(i, (i + 1) % count) for i in range(ends)])  58.2 us
    gather x6, local copies, waits for them, and re-layouts, operate(): jnp.take(flattened, targets, axis=0)  41.8 us
    ppermute x12, waiting for transfers between devices, with_halo(): lax.ppermute(head, axis, [((i + 1) % count, i) for i in range(ends)])  39.4 us
    ppermute x12, starting transfers between devices, with_halo(): lax.ppermute(head, axis, [((i + 1) % count, i) for i in range(ends)])  19.7 us
    dot_general x6, local copies, waits for them, and re-layouts, operate(): jnp.dot(picked, stencil_matrix, preferred_element_type=jnp.float32)  15.5 us
    select_n x7, other arithmetic, operate(): jnp.take(flattened, targets, axis=0)  12.6 us
    another operation x1, local copies, waits for them, and re-layouts, restrict(): paired_block.reshape(height // 2, 2, width, 2, pixels // 4, 4)  10.9 us
  transfers between devices with their start and end apart: 24, of which 12 were waited for; matrix products, arithmetic and copies ran while one was open for 0% of the time, Pallas kernels for 0%

profile of v1, /device:TPU:65, one launch (start us, length us, event | category | flops | bytes accessed | tf_op | source)
XLA Modules:
  0.0 296.2 jit_solution(4314874630144102110)
XLA Ops:
  1.7 4.1 %collective-permute-start = (bf16[1,32,256]{2,1,0:T(8,128)(2,1)S(1)}, bf16[1,32,256]{2,1,0:T(8,128)(2,1)S(1)}, u32[]{:S(2)}, u32[]{:S(2)}) collective-permute-start(bf16[1,32,256]{2,1,0:T(8,128)(2,1)S(1)} %get-tuple-element.27), channel_id=1, source_target_pairs={{0,32},{32,64},{64,96},{96,128},{128,160},{160,192},{192,224},{1,3... | collective-permute-start | bytes 49160 | tf_op jit(solution)/shard_map/ppermute | solution.py:19
  5.8 1.9 collective-permute-start.1
  9.0 1.9 collective-permute-done.1
  10.9 3.2 %collective-permute-start.2 = (bf16[10,1,256]{2,1,0:T(2,128)(2,1)S(1)}, bf16[10,1,256]{2,1,0:T(2,128)(2,1)S(1)}, u32[]{:S(2)}, u32[]{:S(2)}) collective-permute-start(bf16[10,1,256]{2,1,0:T(2,128)(2,1)S(1)} %get-tuple-element.15), channel_id=1, source_target_pairs={{0,1},{1,2},{2,3},{3,4},{4,5},{5,6},{6,7},{7,8},{8,9},{9,10},{10,1... | collective-permute-start | bytes 15368 | tf_op jit(solution)/shard_map/ppermute | solution.py:19
  15.5 3.1 %collective-permute-done.3 = bf16[10,1,256]{2,1,0:T(2,128)(2,1)S(1)} collective-permute-done((bf16[10,1,256]{2,1,0:T(2,128)(2,1)S(1)}, bf16[10,1,256]{2,1,0:T(2,128)(2,1)S(1)}, u32[]{:S(2)}, u32[]{:S(2)}) %collective-permute-start.3) | collective-permute-done | bytes 5152 | tf_op jit(solution)/shard_map/ppermute | solution.py:21
  18.7 6.9 %gather_fusion = bf16[2304,256]{1,0:T(8,128)(2,1)S(1)} fusion(bf16[341,256]{1,0:T(8,128)(2,1)S(1)} %concatenate.56, s32[3072]{0:T(1024)S(1)} %pad_clamp_fusion), kind=kCustom, calls=%fused_computation.clone | custom fusion | bytes 2368512 | tf_op jit(solution)/shard_map/jit(_take)/gather | solution.py:76
  25.6 2.1 broadcast_select_fusion.5
  27.6 2.7 dot_general.30
  30.9 3.4 %collective-permute-start.4 = (bf16[1,32,256]{2,1,0:T(8,128)(2,1)S(1)}, bf16[1,32,256]{2,1,0:T(8,128)(2,1)S(1)}, u32[]{:S(2)}, u32[]{:S(2)}) collective-permute-start(bf16[1,32,256]{2,1,0:T(8,128)(2,1)S(1)} %get-tuple-element.25), channel_id=1, source_target_pairs={{0,32},{32,64},{64,96},{96,128},{128,160},{160,192},{192,224},{1,3... | collective-permute-start | bytes 49160 | tf_op jit(solution)/shard_map/ppermute | solution.py:19
  36.2 3.1 %collective-permute-done.5 = bf16[1,32,256]{2,1,0:T(8,128)(2,1)S(1)} collective-permute-done((bf16[1,32,256]{2,1,0:T(8,128)(2,1)S(1)}, bf16[1,32,256]{2,1,0:T(8,128)(2,1)S(1)}, u32[]{:S(2)}, u32[]{:S(2)}) %collective-permute-start.5) | collective-permute-done | bytes 16416 | tf_op jit(solution)/shard_map/ppermute | solution.py:21
  39.4 3.2 %collective-permute-start.6 = (bf16[10,1,256]{2,1,0:T(2,128)(2,1)S(1)}, bf16[10,1,256]{2,1,0:T(2,128)(2,1)S(1)}, u32[]{:S(2)}, u32[]{:S(2)}) collective-permute-start(bf16[10,1,256]{2,1,0:T(2,128)(2,1)S(1)} %get-tuple-element.13), channel_id=1, source_target_pairs={{0,1},{1,2},{2,3},{3,4},{4,5},{5,6},{6,7},{7,8},{8,9},{9,10},{10,1... | collective-permute-start | bytes 15368 | tf_op jit(solution)/shard_map/ppermute | solution.py:19
  43.9 5.0 %collective-permute-done.7 = bf16[10,1,256]{2,1,0:T(2,128)(2,1)S(1)} collective-permute-done((bf16[10,1,256]{2,1,0:T(2,128)(2,1)S(1)}, bf16[10,1,256]{2,1,0:T(2,128)(2,1)S(1)}, u32[]{:S(2)}, u32[]{:S(2)}) %collective-permute-start.7) | collective-permute-done | bytes 5152 | tf_op jit(solution)/shard_map/ppermute | solution.py:21
  49.0 6.9 %gather_fusion.1 = bf16[2304,256]{1,0:T(8,128)(2,1)S(1)} fusion(bf16[341,256]{1,0:T(8,128)(2,1)S(1)} %concatenate.59, s32[3072]{0:T(1024)S(1)} %pad_clamp_fusion), kind=kCustom, calls=%fused_computation.1.clone | custom fusion | bytes 2368512 | tf_op jit(solution)/shard_map/jit(_take)/gather | solution.py:76
  55.9 2.1 broadcast_select_fusion.4
  57.9 2.7 dot_general.32
  61.8 2.9 collective-permute-start.8
  66.7 3.1 %collective-permute-done.9 = bf16[1,32,256]{2,1,0:T(8,128)(2,1)S(1)} collective-permute-done((bf16[1,32,256]{2,1,0:T(8,128)(2,1)S(1)}, bf16[1,32,256]{2,1,0:T(8,128)(2,1)S(1)}, u32[]{:S(2)}, u32[]{:S(2)}) %collective-permute-start.9) | collective-permute-done | bytes 16416 | tf_op jit(solution)/shard_map/ppermute | solution.py:21
  69.8 9.7 %collective-permute-start.10 = (bf16[10,1,256]{2,1,0:T(2,128)(2,1)S(1)}, bf16[10,1,256]{2,1,0:T(2,128)(2,1)S(1)}, u32[]{:S(2)}, u32[]{:S(2)}) collective-permute-start(bf16[10,1,256]{2,1,0:T(2,128)(2,1)S(1)} %get-tuple-element.11), channel_id=1, source_target_pairs={{0,1},{1,2},{2,3},{3,4},{4,5},{5,6},{6,7},{7,8},{8,9},{9,10},{10,1... | collective-permute-start | bytes 15368 | tf_op jit(solution)/shard_map/ppermute | solution.py:19
  80.8 3.6 %collective-permute-done.11 = bf16[10,1,256]{2,1,0:T(2,128)(2,1)S(1)} collective-permute-done((bf16[10,1,256]{2,1,0:T(2,128)(2,1)S(1)}, bf16[10,1,256]{2,1,0:T(2,128)(2,1)S(1)}, u32[]{:S(2)}, u32[]{:S(2)}) %collective-permute-start.11) | collective-permute-done | bytes 5152 | tf_op jit(solution)/shard_map/ppermute | solution.py:21
  84.5 7.5 %gather_fusion.2 = bf16[2304,256]{1,0:T(8,128)(2,1)} fusion(bf16[341,256]{1,0:T(8,128)(2,1)S(1)} %concatenate.62, s32[3072]{0:T(1024)S(1)} %pad_clamp_fusion), kind=kCustom, calls=%fused_computation.2.clone | custom fusion | bytes 2368512 | tf_op jit(solution)/shard_map/jit(_take)/gather | solution.py:76
  91.9 2.3 broadcast_select_fusion.3
  94.2 2.1 dot_general.34
  98.2 2.9 collective-permute-start.12
  103.1 3.1 %collective-permute-done.13 = bf16[1,32,256]{2,1,0:T(8,128)(2,1)S(1)} collective-permute-done((bf16[1,32,256]{2,1,0:T(8,128)(2,1)S(1)}, bf16[1,32,256]{2,1,0:T(8,128)(2,1)S(1)}, u32[]{:S(2)}, u32[]{:S(2)}) %collective-permute-start.13) | collective-permute-done | bytes 16416 | tf_op jit(solution)/shard_map/ppermute | solution.py:21
  106.2 7.7 %collective-permute-start.14 = (bf16[10,1,256]{2,1,0:T(2,128)(2,1)S(1)}, bf16[10,1,256]{2,1,0:T(2,128)(2,1)S(1)}, u32[]{:S(2)}, u32[]{:S(2)}) collective-permute-start(bf16[10,1,256]{2,1,0:T(2,128)(2,1)S(1)} %get-tuple-element.9), channel_id=1, source_target_pairs={{0,1},{1,2},{2,3},{3,4},{4,5},{5,6},{6,7},{7,8},{8,9},{9,10},{10,1... | collective-permute-start | bytes 15368 | tf_op jit(solution)/shard_map/ppermute | solution.py:19
  115.4 3.4 %collective-permute-done.15 = bf16[10,1,256]{2,1,0:T(2,128)(2,1)S(1)} collective-permute-done((bf16[10,1,256]{2,1,0:T(2,128)(2,1)S(1)}, bf16[10,1,256]{2,1,0:T(2,128)(2,1)S(1)}, u32[]{:S(2)}, u32[]{:S(2)}) %collective-permute-start.15) | collective-permute-done | bytes 5152 | tf_op jit(solution)/shard_map/ppermute | solution.py:21
  118.9 6.9 %gather_fusion.3 = bf16[2304,256]{1,0:T(8,128)(2,1)S(1)} fusion(bf16[341,256]{1,0:T(8,128)(2,1)S(1)} %concatenate.65, s32[3072]{0:T(1024)S(1)} %pad_clamp_fusion), kind=kCustom, calls=%fused_computation.3.clone | custom fusion | bytes 2368512 | tf_op jit(solution)/shard_map/jit(_take)/gather | solution.py:76
  125.8 2.1 broadcast_select_fusion.2
  127.8 2.7 dot_general.36
  131.7 2.9 collective-permute-start.16
  136.5 3.1 %collective-permute-done.17 = bf16[1,32,256]{2,1,0:T(8,128)(2,1)S(1)} collective-permute-done((bf16[1,32,256]{2,1,0:T(8,128)(2,1)S(1)}, bf16[1,32,256]{2,1,0:T(8,128)(2,1)S(1)}, u32[]{:S(2)}, u32[]{:S(2)}) %collective-permute-start.17) | collective-permute-done | bytes 16416 | tf_op jit(solution)/shard_map/ppermute | solution.py:21
  139.7 7.7 %collective-permute-start.18 = (bf16[10,1,256]{2,1,0:T(2,128)(2,1)S(1)}, bf16[10,1,256]{2,1,0:T(2,128)(2,1)S(1)}, u32[]{:S(2)}, u32[]{:S(2)}) collective-permute-start(bf16[10,1,256]{2,1,0:T(2,128)(2,1)S(1)} %get-tuple-element.7), channel_id=1, source_target_pairs={{0,1},{1,2},{2,3},{3,4},{4,5},{5,6},{6,7},{7,8},{8,9},{9,10},{10,1... | collective-permute-start | bytes 15368 | tf_op jit(solution)/shard_map/ppermute | solution.py:19
  148.7 3.5 %collective-permute-done.19 = bf16[10,1,256]{2,1,0:T(2,128)(2,1)S(1)} collective-permute-done((bf16[10,1,256]{2,1,0:T(2,128)(2,1)S(1)}, bf16[10,1,256]{2,1,0:T(2,128)(2,1)S(1)}, u32[]{:S(2)}, u32[]{:S(2)}) %collective-permute-start.19) | collective-permute-done | bytes 5152 | tf_op jit(solution)/shard_map/ppermute | solution.py:21
  152.4 6.9 %gather_fusion.4 = bf16[2304,256]{1,0:T(8,128)(2,1)S(1)} fusion(bf16[341,256]{1,0:T(8,128)(2,1)S(1)} %concatenate.68, s32[3072]{0:T(1024)S(1)} %pad_clamp_fusion), kind=kCustom, calls=%fused_computation.4.clone | custom fusion | bytes 2368512 | tf_op jit(solution)/shard_map/jit(_take)/gather | solution.py:76
  159.2 2.1 broadcast_select_fusion.1
  161.3 2.7 dot_general.38
  164.0 2.5 fusion.7
  166.4 2.9 collective-permute-start.20
  171.3 3.1 %collective-permute-done.21 = bf16[1,32,256]{2,1,0:T(8,128)(2,1)S(1)} collective-permute-done((bf16[1,32,256]{2,1,0:T(8,128)(2,1)S(1)}, bf16[1,32,256]{2,1,0:T(8,128)(2,1)S(1)}, u32[]{:S(2)}, u32[]{:S(2)}) %collective-permute-start.21) | collective-permute-done | bytes 16416 | tf_op jit(solution)/shard_map/ppermute | solution.py:21
  174.4 7.6 %collective-permute-start.22 = (bf16[10,1,256]{2,1,0:T(2,128)(2,1)S(1)}, bf16[10,1,256]{2,1,0:T(2,128)(2,1)S(1)}, u32[]{:S(2)}, u32[]{:S(2)}) collective-permute-start(bf16[10,1,256]{2,1,0:T(2,128)(2,1)S(1)} %get-tuple-element.5), channel_id=1, source_target_pairs={{0,1},{1,2},{2,3},{3,4},{4,5},{5,6},{6,7},{7,8},{8,9},{9,10},{10,1... | collective-permute-start | bytes 15368 | tf_op jit(solution)/shard_map/ppermute | solution.py:19
  183.6 3.3 %collective-permute-done.23 = bf16[10,1,256]{2,1,0:T(2,128)(2,1)S(1)} collective-permute-done((bf16[10,1,256]{2,1,0:T(2,128)(2,1)S(1)}, bf16[10,1,256]{2,1,0:T(2,128)(2,1)S(1)}, u32[]{:S(2)}, u32[]{:S(2)}) %collective-permute-start.23) | collective-permute-done | bytes 5152 | tf_op jit(solution)/shard_map/ppermute | solution.py:21
  187.1 6.9 %gather_fusion.5 = bf16[2304,256]{1,0:T(8,128)(2,1)S(1)} fusion(bf16[341,256]{1,0:T(8,128)(2,1)S(1)} %concatenate.71, s32[3072]{0:T(1024)S(1)} %pad_clamp_fusion), kind=kCustom, calls=%fused_computation.5.clone | custom fusion | bytes 2368512 | tf_op jit(solution)/shard_map/jit(_take)/gather | solution.py:76
  194.0 2.1 broadcast_select_fusion
  196.0 2.7 dot_general.40
  198.8 2.1 fusion
  200.9 10.9 %reshape_reshape.3 = f32[4,2,16,2,64,4]{5,4,3,2,1,0:T(8,128)} reshape(f32[8,32,256]{2,1,0:T(8,128)} %fusion) | data formatting | bytes 524288 | tf_op jit(solution)/shard_map/reshape;reshape | solution.py:31
  211.8 5.7 %reduce_sum.9 = f32[4,2,16,2,64]{4,3,2,1,0:T(2,128)S(1)} reduce(f32[4,2,16,2,64,4]{5,4,3,2,1,0:T(8,128)} %reshape_reshape.3, f32[]{:T(128)} %constant.74.clone.1), dimensions={5}, to_apply=%region_0.2 | reduce | flops 49152 | bytes 327684 | tf_op jit(solution)/shard_map/reduce_sum | solution.py:31
  218.0 76.7 %all_to_all.5 = f32[32,4,16,256]{3,2,1,0:T(8,128)S(1)} all-to-all(f32[32,4,16,256]{3,2,1,0:T(8,128)S(1)} %stack.3), channel_id=1, replica_groups=mesh['frow'=8,'fcol'=32] {'fcol'}, dimensions={0} | all-to-all | bytes 4194304 | tf_op jit(solution)/shard_map/all_to_all | solution.py:84
  (78 shorter events, 27.8 us)
Async XLA Ops:
  0.6 29.7 %copy-start = (bf16[9,256,256]{2,1,0:T(8,128)(2,1)S(1)}, bf16[9,256,256]{2,1,0:T(8,128)(2,1)}, u32[]{:S(2)}) copy-start(bf16[9,256,256]{2,1,0:T(8,128)(2,1)} %param.8) | copy-start | bytes 3538948
  1.7 7.2 %collective-permute-start = (bf16[1,32,256]{2,1,0:T(8,128)(2,1)S(1)}, bf16[1,32,256]{2,1,0:T(8,128)(2,1)S(1)}, u32[]{:S(2)}, u32[]{:S(2)}) collective-permute-start(bf16[1,32,256]{2,1,0:T(8,128)(2,1)S(1)} %get-tuple-element.27), channel_id=1, source_target_pairs={{0,32},{32,64},{64,96},{96,128},{128,160},{160,192},{192,224},{1,3... | collective-permute-start | bytes 49160 | tf_op jit(solution)/shard_map/ppermute | solution.py:19
  5.8 5.1 %collective-permute-start.1 = (bf16[1,32,256]{2,1,0:T(8,128)(2,1)S(1)}, bf16[1,32,256]{2,1,0:T(8,128)(2,1)S(1)}, u32[]{:S(2)}, u32[]{:S(2)}) collective-permute-start(bf16[1,32,256]{2,1,0:T(8,128)(2,1)S(1)} %get-tuple-element.28), channel_id=1, source_target_pairs={{32,0},{64,32},{96,64},{128,96},{160,128},{192,160},{224,192},{33,... | collective-permute-start | bytes 49160 | tf_op jit(solution)/shard_map/ppermute | solution.py:21
  10.9 4.5 %collective-permute-start.2 = (bf16[10,1,256]{2,1,0:T(2,128)(2,1)S(1)}, bf16[10,1,256]{2,1,0:T(2,128)(2,1)S(1)}, u32[]{:S(2)}, u32[]{:S(2)}) collective-permute-start(bf16[10,1,256]{2,1,0:T(2,128)(2,1)S(1)} %get-tuple-element.15), channel_id=1, source_target_pairs={{0,1},{1,2},{2,3},{3,4},{4,5},{5,6},{6,7},{7,8},{8,9},{9,10},{10,1... | collective-permute-start | bytes 15368 | tf_op jit(solution)/shard_map/ppermute | solution.py:19
  14.1 4.4 %collective-permute-start.3 = (bf16[10,1,256]{2,1,0:T(2,128)(2,1)S(1)}, bf16[10,1,256]{2,1,0:T(2,128)(2,1)S(1)}, u32[]{:S(2)}, u32[]{:S(2)}) collective-permute-start(bf16[10,1,256]{2,1,0:T(2,128)(2,1)S(1)} %get-tuple-element.16), channel_id=1, source_target_pairs={{1,0},{2,1},{3,2},{4,3},{5,4},{6,5},{7,6},{8,7},{9,8},{10,9},{11,1... | collective-permute-start | bytes 15368 | tf_op jit(solution)/shard_map/ppermute | solution.py:21
  27.6 2.7 copy-start.1
  27.6 2.7 copy-start.2
  30.9 29.7 %copy-start.3 = (f32[8,32,256]{2,1,0:T(8,128)}, f32[8,32,256]{2,1,0:T(8,128)S(1)}, u32[]{:S(2)}) copy-start(f32[8,32,256]{2,1,0:T(8,128)S(1)} %get-tuple-element.30) | copy-start | bytes 786436
  30.9 5.3 %collective-permute-start.4 = (bf16[1,32,256]{2,1,0:T(8,128)(2,1)S(1)}, bf16[1,32,256]{2,1,0:T(8,128)(2,1)S(1)}, u32[]{:S(2)}, u32[]{:S(2)}) collective-permute-start(bf16[1,32,256]{2,1,0:T(8,128)(2,1)S(1)} %get-tuple-element.25), channel_id=1, source_target_pairs={{0,32},{32,64},{64,96},{96,128},{128,160},{160,192},{192,224},{1,3... | collective-permute-start | bytes 49160 | tf_op jit(solution)/shard_map/ppermute | solution.py:19
  34.3 5.1 %collective-permute-start.5 = (bf16[1,32,256]{2,1,0:T(8,128)(2,1)S(1)}, bf16[1,32,256]{2,1,0:T(8,128)(2,1)S(1)}, u32[]{:S(2)}, u32[]{:S(2)}) collective-permute-start(bf16[1,32,256]{2,1,0:T(8,128)(2,1)S(1)} %get-tuple-element.26), channel_id=1, source_target_pairs={{32,0},{64,32},{96,64},{128,96},{160,128},{192,160},{224,192},{33,... | collective-permute-start | bytes 49160 | tf_op jit(solution)/shard_map/ppermute | solution.py:21
  39.4 4.5 %collective-permute-start.6 = (bf16[10,1,256]{2,1,0:T(2,128)(2,1)S(1)}, bf16[10,1,256]{2,1,0:T(2,128)(2,1)S(1)}, u32[]{:S(2)}, u32[]{:S(2)}) collective-permute-start(bf16[10,1,256]{2,1,0:T(2,128)(2,1)S(1)} %get-tuple-element.13), channel_id=1, source_target_pairs={{0,1},{1,2},{2,3},{3,4},{4,5},{5,6},{6,7},{7,8},{8,9},{9,10},{10,1... | collective-permute-start | bytes 15368 | tf_op jit(solution)/shard_map/ppermute | solution.py:19
  42.6 6.3 %collective-permute-start.7 = (bf16[10,1,256]{2,1,0:T(2,128)(2,1)S(1)}, bf16[10,1,256]{2,1,0:T(2,128)(2,1)S(1)}, u32[]{:S(2)}, u32[]{:S(2)}) collective-permute-start(bf16[10,1,256]{2,1,0:T(2,128)(2,1)S(1)} %get-tuple-element.14), channel_id=1, source_target_pairs={{1,0},{2,1},{3,2},{4,3},{5,4},{6,5},{7,6},{8,7},{9,8},{10,9},{11,1... | collective-permute-start | bytes 15368 | tf_op jit(solution)/shard_map/ppermute | solution.py:21
  61.8 4.9 %collective-permute-start.8 = (bf16[1,32,256]{2,1,0:T(8,128)(2,1)S(1)}, bf16[1,32,256]{2,1,0:T(8,128)(2,1)S(1)}, u32[]{:S(2)}, u32[]{:S(2)}) collective-permute-start(bf16[1,32,256]{2,1,0:T(8,128)(2,1)S(1)} %get-tuple-element.23), channel_id=1, source_target_pairs={{0,32},{32,64},{64,96},{96,128},{128,160},{160,192},{192,224},{1,3... | collective-permute-start | bytes 49160 | tf_op jit(solution)/shard_map/ppermute | solution.py:19
  64.7 5.1 %collective-permute-start.9 = (bf16[1,32,256]{2,1,0:T(8,128)(2,1)S(1)}, bf16[1,32,256]{2,1,0:T(8,128)(2,1)S(1)}, u32[]{:S(2)}, u32[]{:S(2)}) collective-permute-start(bf16[1,32,256]{2,1,0:T(8,128)(2,1)S(1)} %get-tuple-element.24), channel_id=1, source_target_pairs={{32,0},{64,32},{96,64},{128,96},{160,128},{192,160},{224,192},{33,... | collective-permute-start | bytes 49160 | tf_op jit(solution)/shard_map/ppermute | solution.py:21
  69.8 11.0 %collective-permute-start.10 = (bf16[10,1,256]{2,1,0:T(2,128)(2,1)S(1)}, bf16[10,1,256]{2,1,0:T(2,128)(2,1)S(1)}, u32[]{:S(2)}, u32[]{:S(2)}) collective-permute-start(bf16[10,1,256]{2,1,0:T(2,128)(2,1)S(1)} %get-tuple-element.11), channel_id=1, source_target_pairs={{0,1},{1,2},{2,3},{3,4},{4,5},{5,6},{6,7},{7,8},{8,9},{9,10},{10,1... | collective-permute-start | bytes 15368 | tf_op jit(solution)/shard_map/ppermute | solution.py:19
  79.5 4.9 %collective-permute-start.11 = (bf16[10,1,256]{2,1,0:T(2,128)(2,1)S(1)}, bf16[10,1,256]{2,1,0:T(2,128)(2,1)S(1)}, u32[]{:S(2)}, u32[]{:S(2)}) collective-permute-start(bf16[10,1,256]{2,1,0:T(2,128)(2,1)S(1)} %get-tuple-element.12), channel_id=1, source_target_pairs={{1,0},{2,1},{3,2},{4,3},{5,4},{6,5},{7,6},{8,7},{9,8},{10,9},{11,1... | collective-permute-start | bytes 15368 | tf_op jit(solution)/shard_map/ppermute | solution.py:21
  98.2 4.9 %collective-permute-start.12 = (bf16[1,32,256]{2,1,0:T(8,128)(2,1)S(1)}, bf16[1,32,256]{2,1,0:T(8,128)(2,1)S(1)}, u32[]{:S(2)}, u32[]{:S(2)}) collective-permute-start(bf16[1,32,256]{2,1,0:T(8,128)(2,1)S(1)} %get-tuple-element.21), channel_id=1, source_target_pairs={{0,32},{32,64},{64,96},{96,128},{128,160},{160,192},{192,224},{1,3... | collective-permute-start | bytes 49160 | tf_op jit(solution)/shard_map/ppermute | solution.py:19
  101.1 5.1 %collective-permute-start.13 = (bf16[1,32,256]{2,1,0:T(8,128)(2,1)S(1)}, bf16[1,32,256]{2,1,0:T(8,128)(2,1)S(1)}, u32[]{:S(2)}, u32[]{:S(2)}) collective-permute-start(bf16[1,32,256]{2,1,0:T(8,128)(2,1)S(1)} %get-tuple-element.22), channel_id=1, source_target_pairs={{32,0},{64,32},{96,64},{128,96},{160,128},{192,160},{224,192},{33,... | collective-permute-start | bytes 49160 | tf_op jit(solution)/shard_map/ppermute | solution.py:21
  106.2 9.1 %collective-permute-start.14 = (bf16[10,1,256]{2,1,0:T(2,128)(2,1)S(1)}, bf16[10,1,256]{2,1,0:T(2,128)(2,1)S(1)}, u32[]{:S(2)}, u32[]{:S(2)}) collective-permute-start(bf16[10,1,256]{2,1,0:T(2,128)(2,1)S(1)} %get-tuple-element.9), channel_id=1, source_target_pairs={{0,1},{1,2},{2,3},{3,4},{4,5},{5,6},{6,7},{7,8},{8,9},{9,10},{10,1... | collective-permute-start | bytes 15368 | tf_op jit(solution)/shard_map/ppermute | solution.py:19
  113.9 4.9 %collective-permute-start.15 = (bf16[10,1,256]{2,1,0:T(2,128)(2,1)S(1)}, bf16[10,1,256]{2,1,0:T(2,128)(2,1)S(1)}, u32[]{:S(2)}, u32[]{:S(2)}) collective-permute-start(bf16[10,1,256]{2,1,0:T(2,128)(2,1)S(1)} %get-tuple-element.10), channel_id=1, source_target_pairs={{1,0},{2,1},{3,2},{4,3},{5,4},{6,5},{7,6},{8,7},{9,8},{10,9},{11,1... | collective-permute-start | bytes 15368 | tf_op jit(solution)/shard_map/ppermute | solution.py:21
  131.7 4.9 %collective-permute-start.16 = (bf16[1,32,256]{2,1,0:T(8,128)(2,1)S(1)}, bf16[1,32,256]{2,1,0:T(8,128)(2,1)S(1)}, u32[]{:S(2)}, u32[]{:S(2)}) collective-permute-start(bf16[1,32,256]{2,1,0:T(8,128)(2,1)S(1)} %get-tuple-element.19), channel_id=1, source_target_pairs={{0,32},{32,64},{64,96},{96,128},{128,160},{160,192},{192,224},{1,3... | collective-permute-start | bytes 49160 | tf_op jit(solution)/shard_map/ppermute | solution.py:19
  134.6 5.1 %collective-permute-start.17 = (bf16[1,32,256]{2,1,0:T(8,128)(2,1)S(1)}, bf16[1,32,256]{2,1,0:T(8,128)(2,1)S(1)}, u32[]{:S(2)}, u32[]{:S(2)}) collective-permute-start(bf16[1,32,256]{2,1,0:T(8,128)(2,1)S(1)} %get-tuple-element.20), channel_id=1, source_target_pairs={{32,0},{64,32},{96,64},{128,96},{160,128},{192,160},{224,192},{33,... | collective-permute-start | bytes 49160 | tf_op jit(solution)/shard_map/ppermute | solution.py:21
  139.7 9.0 %collective-permute-start.18 = (bf16[10,1,256]{2,1,0:T(2,128)(2,1)S(1)}, bf16[10,1,256]{2,1,0:T(2,128)(2,1)S(1)}, u32[]{:S(2)}, u32[]{:S(2)}) collective-permute-start(bf16[10,1,256]{2,1,0:T(2,128)(2,1)S(1)} %get-tuple-element.7), channel_id=1, source_target_pairs={{0,1},{1,2},{2,3},{3,4},{4,5},{5,6},{6,7},{7,8},{8,9},{9,10},{10,1... | collective-permute-start | bytes 15368 | tf_op jit(solution)/shard_map/ppermute | solution.py:19
  147.4 4.9 %collective-permute-start.19 = (bf16[10,1,256]{2,1,0:T(2,128)(2,1)S(1)}, bf16[10,1,256]{2,1,0:T(2,128)(2,1)S(1)}, u32[]{:S(2)}, u32[]{:S(2)}) collective-permute-start(bf16[10,1,256]{2,1,0:T(2,128)(2,1)S(1)} %get-tuple-element.8), channel_id=1, source_target_pairs={{1,0},{2,1},{3,2},{4,3},{5,4},{6,5},{7,6},{8,7},{9,8},{10,9},{11,1... | collective-permute-start | bytes 15368 | tf_op jit(solution)/shard_map/ppermute | solution.py:21
  166.4 4.9 %collective-permute-start.20 = (bf16[1,32,256]{2,1,0:T(8,128)(2,1)S(1)}, bf16[1,32,256]{2,1,0:T(8,128)(2,1)S(1)}, u32[]{:S(2)}, u32[]{:S(2)}) collective-permute-start(bf16[1,32,256]{2,1,0:T(8,128)(2,1)S(1)} %get-tuple-element.17), channel_id=1, source_target_pairs={{0,32},{32,64},{64,96},{96,128},{128,160},{160,192},{192,224},{1,3... | collective-permute-start | bytes 49160 | tf_op jit(solution)/shard_map/ppermute | solution.py:19
  169.4 5.1 %collective-permute-start.21 = (bf16[1,32,256]{2,1,0:T(8,128)(2,1)S(1)}, bf16[1,32,256]{2,1,0:T(8,128)(2,1)S(1)}, u32[]{:S(2)}, u32[]{:S(2)}) collective-permute-start(bf16[1,32,256]{2,1,0:T(8,128)(2,1)S(1)} %get-tuple-element.18), channel_id=1, source_target_pairs={{32,0},{64,32},{96,64},{128,96},{160,128},{192,160},{224,192},{33,... | collective-permute-start | bytes 49160 | tf_op jit(solution)/shard_map/ppermute | solution.py:21
  174.4 9.2 %collective-permute-start.22 = (bf16[10,1,256]{2,1,0:T(2,128)(2,1)S(1)}, bf16[10,1,256]{2,1,0:T(2,128)(2,1)S(1)}, u32[]{:S(2)}, u32[]{:S(2)}) collective-permute-start(bf16[10,1,256]{2,1,0:T(2,128)(2,1)S(1)} %get-tuple-element.5), channel_id=1, source_target_pairs={{0,1},{1,2},{2,3},{3,4},{4,5},{5,6},{6,7},{7,8},{8,9},{9,10},{10,1... | collective-permute-start | bytes 15368 | tf_op jit(solution)/shard_map/ppermute | solution.py:19
  182.1 4.8 %collective-permute-start.23 = (bf16[10,1,256]{2,1,0:T(2,128)(2,1)S(1)}, bf16[10,1,256]{2,1,0:T(2,128)(2,1)S(1)}, u32[]{:S(2)}, u32[]{:S(2)}) collective-permute-start(bf16[10,1,256]{2,1,0:T(2,128)(2,1)S(1)} %get-tuple-element.6), channel_id=1, source_target_pairs={{1,0},{2,1},{3,2},{4,3},{5,4},{6,5},{7,6},{8,7},{9,8},{10,9},{11,1... | collective-permute-start | bytes 15368 | tf_op jit(solution)/shard_map/ppermute | solution.py:21
  196.0 2.7 copy-start.4
